TPU v7x, 32 devices: a whole 2x2x4 slice. The times are simulated.
32 devices in a mesh: row: 8 (over z, x), col: 4 (over y, core).
Axes of the slice: x: 2, y: 2, z: 4, core: 2. Of those that a mesh axis runs over, the one named last changes fastest.
Arguments:
- obj_re: float32 [1024, 512], P('row', 'col'), may hold values from -6 to 6
- obj_im: float32 [1024, 512], P('row', 'col'), may hold values from -6 to 6
- probe_re: float32 [4, 256, 256], replicated, may hold values from -3 to 3
- probe_im: float32 [4, 256, 256], replicated, may hold values from -3 to 3
- amps: float32 [8, 4, 1, 256, 256], P('row', 'col'), may hold values from 0.2 to 4
- positions: int32 [8, 4, 1, 2], P('row', 'col'), may hold values from -128 to 896, as said below
Outputs:
- new_obj_re: float32 [1024, 512], P('row', 'col')
- new_obj_im: float32 [1024, 512], P('row', 'col')
- new_probe_re: float32 [4, 256, 256], replicated
- new_probe_im: float32 [4, 256, 256], replicated
Inputs may be any that keep to these rules, and one draw needn't show every extreme that they name: `positions`: each position's offsets are multiples of 64. A position stored at [i, j, p] has its row r with i * 128 - 256 // 2 <= r <= (i + 1) * 128 - 256 // 2 and its column c with j * 128 - 256 // 2 <= c <= (j + 1) * 128 - 256 // 2.
All inputs are finite; a program needn't handle non-finite values.
Results may differ from a plain program's by a relative error of at most 0.0055.
Values sent between devices are 32-bit elements; how exact they have to be, the bound alone decides.
No kernel may reach another device: no remote copies, remote signals or barrier semaphores. Data moves between devices by JAX's collectives and lax.ppermute only.
A program may use at most 64 MiB of HBM per device.

v0:
```python
import math
import jax
import jax.numpy as jnp
from jax import lax
from jax.sharding import PartitionSpec as P

ITERS = 3
amp_floor = 0.25
light_ratio = 0.1
mass_ratio = 0.1
probe_step = 6.0


def passed_along(array, axis, by):
    devices = lax.axis_size(axis)
    pairs = [(i, i + by) for i in range(devices) if 0 <= i + by < devices]
    return lax.ppermute(array, axis, pairs)


def with_halo(cells, sides, width):
    for axis, dim in sides:
        count = lax.axis_size(axis)
        ends = count - 1
        head = lax.slice_in_dim(cells, 0, width, axis=dim)
        tail = lax.slice_in_dim(cells, cells.shape[dim] - width, cells.shape[dim], axis=dim)
        cells = jnp.concatenate(
            [
                lax.ppermute(tail, axis, [(i, (i + 1) % count) for i in range(ends)]),
                cells,
                lax.ppermute(head, axis, [((i + 1) % count, i) for i in range(ends)]),
            ],
            axis=dim,
        )
    return cells


def make_tables(width, sign):
    index = jnp.arange(width, dtype=jnp.int32)
    turns = index[:, None] * index[None, :] % width
    angle = turns.astype(jnp.float32) * (2.0 * math.pi / width)
    real = (jnp.cos(angle) / math.sqrt(width)).astype(jnp.bfloat16)
    imag = (sign * jnp.sin(angle) / math.sqrt(width)).astype(jnp.bfloat16)
    right_pair = jnp.concatenate(
        [jnp.concatenate([real, imag], 1), jnp.concatenate([-imag, real], 1)], 0
    )
    return (right_pair, real, imag)


def transform(wave, table):
    right_pair, real, imag = table
    width = real.shape[0]
    half = jnp.einsum("mnc,cd->mnd", wave, right_pair, preferred_element_type=jnp.float32).astype(
        jnp.bfloat16
    )
    first = jnp.einsum("kn,mnd->mkd", real, half, preferred_element_type=jnp.float32)
    second = jnp.einsum("kn,mnd->mkd", imag, half, preferred_element_type=jnp.float32)
    return (first[..., :width] - second[..., width:], first[..., width:] + second[..., :width])


def one_view(window, probe_re, probe_im, view, forward, backward):
    win_re = window[0][None]
    win_im = window[1][None]
    psi = jnp.concatenate(
        [probe_re * win_re - probe_im * win_im, probe_re * win_im + probe_im * win_re], axis=2
    ).astype(jnp.bfloat16)
    spec_re, spec_im = transform(psi, forward)
    modulus = jnp.sqrt(jnp.sum(spec_re * spec_re + spec_im * spec_im, axis=0))
    factor = view / jnp.maximum(modulus, amp_floor) - 1.0
    change = jnp.concatenate([spec_re * factor, spec_im * factor], axis=2).astype(jnp.bfloat16)
    return transform(change, backward)


def place(buffer, piece, row_at, col_at):
    start = (jnp.int32(0), row_at, col_at)
    return lax.dynamic_update_slice(buffer, piece, start)


def send_rows(strip, offset):
    return passed_along(strip, "row", offset)


def send_cols(strip, offset):
    return passed_along(strip, "col", offset)


def fold_back(buffer, rows, cols, rim):
    middle = buffer[:, rim : rim + rows]
    from_below = send_rows(buffer[:, :rim], -1)
    from_above = send_rows(buffer[:, rim + rows :], 1)
    middle = middle.at[:, rows - rim :].add(from_below)
    middle = middle.at[:, :rim].add(from_above)
    core = middle[:, :, rim : rim + cols]
    from_right = send_cols(middle[:, :, :rim], -1)
    from_left = send_cols(middle[:, :, rim + cols :], 1)
    core = core.at[:, :, cols - rim :].add(from_right)
    return core.at[:, :, :rim].add(from_left)


def local(obj_re, obj_im, probe_re, probe_im, amps, positions):
    rows, cols = obj_re.shape
    modes, width = (probe_re.shape[0], probe_re.shape[1])
    rim = width // 2
    forward = make_tables(width, -1.0)
    backward = make_tables(width, 1.0)
    spots = positions[0, 0]
    views = amps[0, 0]
    my_row = lax.axis_index("row")
    my_col = lax.axis_index("col")
    row_base = my_row * rows - rim
    col_base = my_col * cols - rim
    local_rows = spots[:, 0] - row_base
    local_cols = spots[:, 1] - col_base
    wide_rows = rows + 2 * rim
    wide_cols = cols + 2 * rim
    power = jnp.sum(probe_re * probe_re + probe_im * probe_im, axis=0)
    light_buf = jnp.zeros((1, wide_rows, wide_cols), jnp.float32)
    slot = 0
    light_buf = place(light_buf, power[None], local_rows[slot], local_cols[slot])
    light = fold_back(light_buf, rows, cols, rim)[0]
    peak = lax.pmax(jnp.max(light), ("row", "col"))
    denom = light + light_ratio * peak
    state = jnp.stack([obj_re, obj_im])
    grad_re = jnp.zeros((modes, width, width), jnp.float32)
    grad_im = jnp.zeros((modes, width, width), jnp.float32)
    mass = jnp.zeros((width, width), jnp.float32)
    for step in range(ITERS):
        extended = with_halo(state, (("row", 1), ("col", 2)), rim)
        buffer = jnp.zeros((2, wide_rows, wide_cols), jnp.float32)
        last_pass = step == ITERS - 1
        slot = 0
        window = lax.dynamic_slice(
            extended, (jnp.int32(0), local_rows[slot], local_cols[slot]), (2, width, width)
        )
        exit_re, exit_im = one_view(window, probe_re, probe_im, views[slot], forward, backward)
        obj_grad = jnp.stack(
            [
                jnp.sum(probe_re * exit_re + probe_im * exit_im, axis=0),
                jnp.sum(probe_re * exit_im - probe_im * exit_re, axis=0),
            ]
        )
        buffer = place(buffer, obj_grad, local_rows[slot], local_cols[slot])
        if last_pass:
            win_re = window[0][None]
            win_im = window[1][None]
            grad_re = win_re * exit_re + win_im * exit_im
            grad_im = win_re * exit_im - win_im * exit_re
            mass = window[0] * window[0] + window[1] * window[1]
        state = state + fold_back(buffer, rows, cols, rim) / denom[None]
    pixels = width * width
    terms = jnp.concatenate(
        [grad_re.reshape(modes, pixels), grad_im.reshape(modes, pixels), mass.reshape(1, pixels)],
        axis=0,
    )
    probe_flat = jnp.concatenate(
        [probe_re.reshape(modes, pixels), probe_im.reshape(modes, pixels)], axis=0
    )
    summed = lax.psum(terms, ("row", "col"))
    scale = probe_step / (summed[2 * modes] + mass_ratio * jnp.mean(summed[2 * modes]))
    updated = probe_flat + summed[: 2 * modes] * scale[None]
    new_re = updated[:modes].reshape(modes, width, width)
    new_im = updated[modes:].reshape(modes, width, width)
    return (state[0], state[1], new_re, new_im)


def solution(mesh):
    placed = (
        P("row", "col"),
        P("row", "col"),
        P(),
        P(),
        P("row", "col", None, None, None),
        P("row", "col", None, None),
    )
    return jax.shard_map(
        local,
        mesh=mesh,
        in_specs=placed,
        out_specs=(P("row", "col"), P("row", "col"), P(), P()),
        check_vma=False,
    )
```

profile of v0, /device:TPU:0, one launch (start us, length us, event | category | flops | bytes accessed | tf_op | source)
XLA Modules:
  0.0 428.3 jit_solution(1866094221004445587)
XLA Ops:
  8.3 4.9 %collective-permute-start = (f32[2,128,128]{2,1,0:T(8,128)S(1)}, f32[2,128,128]{2,1,0:T(8,128)S(1)}, u32[]{:S(2)}, u32[]{:S(2)}) collective-permute-start(f32[2,128,128]{2,1,0:T(8,128)S(1)} %pad_maximum_fusion.11), channel_id=1, source_target_pairs={{0,4},{4,8},{8,12},{12,16},{16,20},{20,24},{24,28},{1,5},{5,9},{9,... | collective-permute-start | bytes 393224 | tf_op jit(solution)/shard_map/ppermute | solution.py:28
  14.4 1.6 fusion.77
  16.1 3.9 collective-permute-done.1
  20.0 1.7 pad_maximum_fusion.8
  21.7 2.0 collective-permute-start.2
  32.4 1.6 multiply_convert_fusion.7
  34.1 1.8 fusion.32
  37.8 1.4 convolution_bitcast_fusion.10
  42.2 2.8 convolution_bitcast_fusion.8
  45.0 2.7 convolution_bitcast_fusion.9
  48.6 2.6 dynamic_update_slice.13
  51.2 1.8 fusion.151
  54.3 5.7 %collective-permute-start.9 = (f32[1,128,384]{2,1,0:T(8,128)}, f32[1,128,384]{2,1,0:T(8,128)}, u32[]{:S(2)}, u32[]{:S(2)}) collective-permute-start(f32[1,128,384]{2,1,0:T(8,128)} %get-tuple-element.356), channel_id=1, source_target_pairs={{0,4},{4,8},{8,12},{12,16},{16,20},{20,24},{24,28},{1,5},{5,9},{9,... | collective-permute-start | bytes 589832 | tf_op jit(solution)/shard_map/ppermute | solution.py:17
  59.9 3.0 add_reduce_fusion.5
  63.8 2.1 copy.48
  67.0 4.5 %dynamic_update_slice.12 = f32[2,384,384]{2,1,0:T(8,128)} dynamic-update-slice(f32[2,384,384]{2,1,0:T(8,128)} %broadcast.616.clone, f32[2,256,256]{2,1,0:T(8,128)} %copy.48, s32[]{:T(128)} %constant.548.clone.1, s32[]{:T(128)S(6)} %select_n.65, s32[]{:T(128)S(6)} %select_n.66) | dynamic-update-slice | bytes 1048580 | tf_op jit(solution)/shard_map/dynamic_update_slice | solution.py:75
  71.5 2.1 fusion.150
  74.9 5.5 %collective-permute-start.5 = (f32[2,128,384]{2,1,0:T(8,128)}, f32[2,128,384]{2,1,0:T(8,128)}, u32[]{:S(2)}, u32[]{:S(2)}) collective-permute-start(f32[2,128,384]{2,1,0:T(8,128)} %get-tuple-element.354), channel_id=1, source_target_pairs={{0,4},{4,8},{8,12},{12,16},{16,20},{20,24},{24,28},{1,5},{5,9},{9,... | collective-permute-start | bytes 1179656 | tf_op jit(solution)/shard_map/ppermute | solution.py:17
  82.9 3.8 collective-permute-start.11
  88.2 46.3 %pmax.7 = f32[]{:T(128)} all-reduce(f32[]{:T(128)} %fusion.146), channel_id=1, replica_groups=mesh['row'=8,'col'=4] {'row','col'}, use_global_device_ids=true, to_apply=%region_5.6 | all-reduce | flops 1 | bytes 8 | tf_op jit(solution)/shard_map/pmax | solution.py:120
  137.8 3.0 collective-permute-start.7
  142.7 4.2 collective-permute-start.12
  148.2 2.6 collective-permute-done.12
  150.8 4.4 %collective-permute-done.13 = f32[2,128,128]{2,1,0:T(8,128)S(1)} collective-permute-done((f32[2,128,128]{2,1,0:T(8,128)S(1)}, f32[2,128,128]{2,1,0:T(8,128)S(1)}, u32[]{:S(2)}, u32[]{:S(2)}) %collective-permute-start.13) | collective-permute-done | bytes 131104 | tf_op jit(solution)/shard_map/ppermute | solution.py:30
  155.2 2.0 collective-permute-start.14
  158.6 3.8 collective-permute-done.15
  174.1 5.9 %dynamic_update_slice.14 = f32[2,384,384]{2,1,0:T(8,128)S(1)} dynamic-update-slice(f32[2,384,384]{2,1,0:T(8,128)S(1)} %broadcast.616.clone.1, f32[2,256,256]{2,1,0:T(8,128)} %copy.58, s32[]{:T(128)} %constant.548.clone.1, s32[]{:T(128)S(6)} %select_n.65, s32[]{:T(128)S(6)} %select_n.66) | dynamic-update-slice | bytes 1048580 | tf_op jit(solution)/shard_map/dynamic_update_slice | solution.py:75
  181.5 5.5 %collective-permute-start.17 = (f32[2,128,384]{2,1,0:T(8,128)S(1)}, f32[2,128,384]{2,1,0:T(8,128)S(1)}, u32[]{:S(2)}, u32[]{:S(2)}) collective-permute-start(f32[2,128,384]{2,1,0:T(8,128)S(1)} %get-tuple-element.352), channel_id=1, source_target_pairs={{0,4},{4,8},{8,12},{12,16},{16,20},{20,24},{24,28},{1,5},{5,9},{9,... | collective-permute-start | bytes 1179656 | tf_op jit(solution)/shard_map/ppermute | solution.py:17
  186.9 3.8 collective-permute-done.16
  190.7 12.4 %collective-permute-done.17 = f32[2,128,384]{2,1,0:T(8,128)S(1)} collective-permute-done((f32[2,128,384]{2,1,0:T(8,128)S(1)}, f32[2,128,384]{2,1,0:T(8,128)S(1)}, u32[]{:S(2)}, u32[]{:S(2)}) %collective-permute-start.17) | collective-permute-done | bytes 393248 | tf_op jit(solution)/shard_map/ppermute | solution.py:17
  204.5 3.3 collective-permute-start.19
  208.9 4.1 collective-permute-start.20
  215.5 4.4 %collective-permute-done.21 = f32[2,128,128]{2,1,0:T(8,128)S(1)} collective-permute-done((f32[2,128,128]{2,1,0:T(8,128)S(1)}, f32[2,128,128]{2,1,0:T(8,128)S(1)}, u32[]{:S(2)}, u32[]{:S(2)}) %collective-permute-start.21) | collective-permute-done | bytes 131104 | tf_op jit(solution)/shard_map/ppermute | solution.py:30
  219.9 3.2 collective-permute-start.22
  223.1 1.5 collective-permute-start.23
  224.6 5.7 %collective-permute-done.23 = f32[2,384,128]{2,1,0:T(8,128)S(1)} collective-permute-done((f32[2,384,128]{2,1,0:T(8,128)S(1)}, f32[2,384,128]{2,1,0:T(8,128)S(1)}, u32[]{:S(2)}, u32[]{:S(2)}) %collective-permute-start.23) | collective-permute-done | bytes 393248 | tf_op jit(solution)/shard_map/ppermute | solution.py:30
  241.2 1.6 copy.86
  242.9 1.6 copy.85
  245.7 5.9 %dynamic_update_slice.15 = f32[2,384,384]{2,1,0:T(8,128)S(1)} dynamic-update-slice(f32[2,384,384]{2,1,0:T(8,128)S(1)} %broadcast.616, f32[2,256,256]{2,1,0:T(8,128)} %pad_maximum_fusion.7, s32[]{:T(128)} %constant.548.clone.1, s32[]{:T(128)S(6)} %select_n.65, s32[]{:T(128)S(6)} %select_n.66) | dynamic-update-slice | bytes 1048580 | tf_op jit(solution)/shard_map/dynamic_update_slice | solution.py:75
  253.9 5.5 %collective-permute-start.25 = (f32[2,128,384]{2,1,0:T(8,128)}, f32[2,128,384]{2,1,0:T(8,128)}, u32[]{:S(2)}, u32[]{:S(2)}) collective-permute-start(f32[2,128,384]{2,1,0:T(8,128)} %get-tuple-element.350), channel_id=1, source_target_pairs={{0,4},{4,8},{8,12},{12,16},{16,20},{20,24},{24,28},{1,5},{5,9},{9,... | collective-permute-start | bytes 1179656 | tf_op jit(solution)/shard_map/ppermute | solution.py:17
  259.4 3.9 pad_maximum_fusion
  263.4 10.7 %collective-permute-done.25 = f32[2,128,384]{2,1,0:T(8,128)} collective-permute-done((f32[2,128,384]{2,1,0:T(8,128)}, f32[2,128,384]{2,1,0:T(8,128)}, u32[]{:S(2)}, u32[]{:S(2)}) %collective-permute-start.25) | collective-permute-done | bytes 393248 | tf_op jit(solution)/shard_map/ppermute | solution.py:17
  276.6 6.9 %collective-permute-start.27 = (f32[2,128,128]{2,1,0:T(8,128)S(1)}, f32[2,128,128]{2,1,0:T(8,128)S(1)}, u32[]{:S(2)}, u32[]{:S(2)}) collective-permute-start(f32[2,128,128]{2,1,0:T(8,128)S(1)} %get-tuple-element.365), channel_id=1, source_target_pairs={{0,1},{1,2},{2,3},{4,5},{5,6},{6,7},{8,9},{9,10},{10,11},{12,13},{... | collective-permute-start | bytes 393224 | tf_op jit(solution)/shard_map/ppermute | solution.py:17
  284.2 1.6 copy.84
  286.6 124.2 %all-reduce.2.cloned.1.call-done = f32[9,65536]{1,0:T(8,128)} async-done(((f32[9,65536]{1,0:T(8,128)}), f32[9,65536]{1,0:T(8,128)}) %all-reduce.2.cloned.1.call-update) | async-done | bytes 2359312 | tf_op jit(solution)/shard_map/psum | solution.py:157
  410.8 2.7 slice_reduce_fusion
  414.2 1.9 add_divide_fusion
  416.0 2.5 fusion
  (169 shorter events, 69.7 us)
Async XLA Ops:
  7.2 21.6 %copy-start = (f32[4,256,256]{2,1,0:T(8,128)S(1)}, f32[4,256,256]{2,1,0:T(8,128)}, u32[]{:S(2)}) copy-start(f32[4,256,256]{2,1,0:T(8,128)} %param.72) | copy-start | bytes 3145732
  7.2 21.9 %copy-start.1 = (f32[4,256,256]{2,1,0:T(8,128)S(1)}, f32[4,256,256]{2,1,0:T(8,128)}, u32[]{:S(2)}) copy-start(f32[4,256,256]{2,1,0:T(8,128)} %param.73) | copy-start | bytes 3145732
  7.2 403.6 %all-reduce.2.cloned.1.call-start = ((), (), s32[]{:S(2)}) async-start(), calls=%async_computation | async-start | bytes 8388608 | tf_op jit(solution)/shard_map/psum | solution.py:157
  8.3 7.8 %collective-permute-start = (f32[2,128,128]{2,1,0:T(8,128)S(1)}, f32[2,128,128]{2,1,0:T(8,128)S(1)}, u32[]{:S(2)}, u32[]{:S(2)}) collective-permute-start(f32[2,128,128]{2,1,0:T(8,128)S(1)} %pad_maximum_fusion.11), channel_id=1, source_target_pairs={{0,4},{4,8},{8,12},{12,16},{16,20},{20,24},{24,28},{1,5},{5,9},{9,... | collective-permute-start | bytes 393224 | tf_op jit(solution)/shard_map/ppermute | solution.py:28
  13.1 6.9 %collective-permute-start.1 = (f32[2,128,128]{2,1,0:T(8,128)S(1)}, f32[2,128,128]{2,1,0:T(8,128)S(1)}, u32[]{:S(2)}, u32[]{:S(2)}) collective-permute-start(f32[2,128,128]{2,1,0:T(8,128)S(1)} %pad_maximum_fusion.11), channel_id=1, source_target_pairs={{4,0},{8,4},{12,8},{16,12},{20,16},{24,20},{28,24},{5,1},{9,5},{13... | collective-permute-start | bytes 393224 | tf_op jit(solution)/shard_map/ppermute | solution.py:30
  16.1 3.9 copy-start.14
  20.0 1.7 copy-start.15
  21.7 12.4 %collective-permute-start.2 = (f32[2,384,128]{2,1,0:T(8,128)}, f32[2,384,128]{2,1,0:T(8,128)}, u32[]{:S(2)}, u32[]{:S(2)}) collective-permute-start(f32[2,384,128]{2,1,0:T(8,128)} %pad_maximum_fusion.8), channel_id=1, source_target_pairs={{0,1},{1,2},{2,3},{4,5},{5,6},{6,7},{8,9},{9,10},{10,11},{12,13},{... | collective-permute-start | bytes 1179656 | tf_op jit(solution)/shard_map/ppermute | solution.py:28
  23.7 10.4 %collective-permute-start.3 = (f32[2,384,128]{2,1,0:T(8,128)}, f32[2,384,128]{2,1,0:T(8,128)}, u32[]{:S(2)}, u32[]{:S(2)}) collective-permute-start(f32[2,384,128]{2,1,0:T(8,128)} %pad_maximum_fusion.8), channel_id=1, source_target_pairs={{1,0},{2,1},{3,2},{5,4},{6,5},{7,6},{9,8},{10,9},{11,10},{13,12},{... | collective-permute-start | bytes 1179656 | tf_op jit(solution)/shard_map/ppermute | solution.py:30
  28.7 5.4 %copy-start.9 = (f32[128,128]{1,0:T(8,128)S(1)}, f32[128,128]{1,0:T(8,128)}, u32[]{:S(2)}) copy-start(f32[128,128]{1,0:T(8,128)} %param.71) | copy-start | bytes 196612
  28.8 5.4 %copy-start.10 = (f32[128,128]{1,0:T(8,128)S(1)}, f32[128,128]{1,0:T(8,128)}, u32[]{:S(2)}) copy-start(f32[128,128]{1,0:T(8,128)} %param.70) | copy-start | bytes 196612
  31.4 10.1 %copy-start.19 = (bf16[256,256]{1,0:T(8,128)(2,1)}, bf16[256,256]{1,0:T(8,128)(2,1)S(1)}, u32[]{:S(2)}) copy-start(bf16[256,256]{1,0:T(8,128)(2,1)S(1)} %fusion.78) | copy-start | bytes 393220
  32.4 9.1 %copy-start.22 = (bf16[256,256]{1,0:T(8,128)(2,1)}, bf16[256,256]{1,0:T(8,128)(2,1)S(1)}, u32[]{:S(2)}) copy-start(bf16[256,256]{1,0:T(8,128)(2,1)S(1)} %multiply_convert_fusion.6) | copy-start | bytes 393220
  34.1 3.0 copy-start.28
  34.1 7.4 %copy-start.25 = (bf16[256,256]{1,0:T(8,128)(2,1)}, bf16[256,256]{1,0:T(8,128)(2,1)S(1)}, u32[]{:S(2)}) copy-start(bf16[256,256]{1,0:T(8,128)(2,1)S(1)} %get-tuple-element.377) | copy-start | bytes 393220
  53.0 27.5 %collective-permute-start.8 = (f32[1,128,384]{2,1,0:T(8,128)}, f32[1,128,384]{2,1,0:T(8,128)}, u32[]{:S(2)}, u32[]{:S(2)}) collective-permute-start(f32[1,128,384]{2,1,0:T(8,128)} %get-tuple-element.355), channel_id=1, source_target_pairs={{4,0},{8,4},{12,8},{16,12},{20,16},{24,20},{28,24},{5,1},{9,5},{13... | collective-permute-start | bytes 589832 | tf_op jit(solution)/shard_map/ppermute | solution.py:17
  54.3 26.2 %collective-permute-start.9 = (f32[1,128,384]{2,1,0:T(8,128)}, f32[1,128,384]{2,1,0:T(8,128)}, u32[]{:S(2)}, u32[]{:S(2)}) collective-permute-start(f32[1,128,384]{2,1,0:T(8,128)} %get-tuple-element.356), channel_id=1, source_target_pairs={{0,4},{4,8},{8,12},{12,16},{16,20},{20,24},{24,28},{1,5},{5,9},{9,... | collective-permute-start | bytes 589832 | tf_op jit(solution)/shard_map/ppermute | solution.py:17
  73.6 61.6 %collective-permute-start.4 = (f32[2,128,384]{2,1,0:T(8,128)}, f32[2,128,384]{2,1,0:T(8,128)}, u32[]{:S(2)}, u32[]{:S(2)}) collective-permute-start(f32[2,128,384]{2,1,0:T(8,128)} %get-tuple-element.353), channel_id=1, source_target_pairs={{4,0},{8,4},{12,8},{16,12},{20,16},{24,20},{28,24},{5,1},{9,5},{13... | collective-permute-start | bytes 1179656 | tf_op jit(solution)/shard_map/ppermute | solution.py:17
  74.9 60.3 %collective-permute-start.5 = (f32[2,128,384]{2,1,0:T(8,128)}, f32[2,128,384]{2,1,0:T(8,128)}, u32[]{:S(2)}, u32[]{:S(2)}) collective-permute-start(f32[2,128,384]{2,1,0:T(8,128)} %get-tuple-element.354), channel_id=1, source_target_pairs={{0,4},{4,8},{8,12},{12,16},{16,20},{20,24},{24,28},{1,5},{5,9},{9,... | collective-permute-start | bytes 1179656 | tf_op jit(solution)/shard_map/ppermute | solution.py:17
  81.6 6.0 %copy-start.8 = (f32[1,128,384]{2,1,0:T(8,128)}, f32[1,128,384]{2,1,0:T(8,128)S(1)}, u32[]{:S(2)}) copy-start(f32[1,128,384]{2,1,0:T(8,128)S(1)} %fusion.48) | copy-start | bytes 589828
  81.6 5.1 %collective-permute-start.10 = (f32[1,128,128]{2,1,0:T(8,128)S(1)}, f32[1,128,128]{2,1,0:T(8,128)S(1)}, u32[]{:S(2)}, u32[]{:S(2)}) collective-permute-start(f32[1,128,128]{2,1,0:T(8,128)S(1)} %get-tuple-element.370), channel_id=1, source_target_pairs={{1,0},{2,1},{3,2},{5,4},{6,5},{7,6},{9,8},{10,9},{11,10},{13,12},{... | collective-permute-start | bytes 196616 | tf_op jit(solution)/shard_map/ppermute | solution.py:17
  82.9 4.7 %collective-permute-start.11 = (f32[1,128,128]{2,1,0:T(8,128)S(1)}, f32[1,128,128]{2,1,0:T(8,128)S(1)}, u32[]{:S(2)}, u32[]{:S(2)}) collective-permute-start(f32[1,128,128]{2,1,0:T(8,128)S(1)} %get-tuple-element.371), channel_id=1, source_target_pairs={{0,1},{1,2},{2,3},{4,5},{5,6},{6,7},{8,9},{9,10},{10,11},{12,13},{... | collective-permute-start | bytes 196616 | tf_op jit(solution)/shard_map/ppermute | solution.py:17
  136.5 5.2 %collective-permute-start.6 = (f32[2,128,128]{2,1,0:T(8,128)S(1)}, f32[2,128,128]{2,1,0:T(8,128)S(1)}, u32[]{:S(2)}, u32[]{:S(2)}) collective-permute-start(f32[2,128,128]{2,1,0:T(8,128)S(1)} %get-tuple-element.368), channel_id=1, source_target_pairs={{1,0},{2,1},{3,2},{5,4},{6,5},{7,6},{9,8},{10,9},{11,10},{13,12},{... | collective-permute-start | bytes 393224 | tf_op jit(solution)/shard_map/ppermute | solution.py:17
  137.8 4.0 collective-permute-start.7
  141.7 9.1 %copy-start.11 = (f32[128,128]{1,0:T(8,128)}, f32[128,128]{1,0:T(8,128)S(1)}, u32[]{:S(2)}) copy-start(f32[128,128]{1,0:T(8,128)S(1)} %add_bitcast_fusion.2) | copy-start | bytes 196612
  142.7 20.6 %copy-start.6 = (f32[2,128,128]{2,1,0:T(8,128)}, f32[2,128,128]{2,1,0:T(8,128)S(1)}, u32[]{:S(2)}) copy-start(f32[2,128,128]{2,1,0:T(8,128)S(1)} %fusion.63) | copy-start | bytes 393220
  142.7 8.1 %collective-permute-start.12 = (f32[2,128,128]{2,1,0:T(8,128)S(1)}, f32[2,128,128]{2,1,0:T(8,128)S(1)}, u32[]{:S(2)}, u32[]{:S(2)}) collective-permute-start(f32[2,128,128]{2,1,0:T(8,128)S(1)} %fusion.63), channel_id=1, source_target_pairs={{0,4},{4,8},{8,12},{12,16},{16,20},{20,24},{24,28},{1,5},{5,9},{9,... | collective-permute-start | bytes 393224 | tf_op jit(solution)/shard_map/ppermute | solution.py:28
  146.9 8.2 %collective-permute-start.13 = (f32[2,128,128]{2,1,0:T(8,128)S(1)}, f32[2,128,128]{2,1,0:T(8,128)S(1)}, u32[]{:S(2)}, u32[]{:S(2)}) collective-permute-start(f32[2,128,128]{2,1,0:T(8,128)S(1)} %fusion.63), channel_id=1, source_target_pairs={{4,0},{8,4},{12,8},{16,12},{20,16},{24,20},{28,24},{5,1},{9,5},{13... | collective-permute-start | bytes 393224 | tf_op jit(solution)/shard_map/ppermute | solution.py:30
  155.2 3.4 collective-permute-start.14
  157.2 5.1 %collective-permute-start.15 = (f32[2,384,128]{2,1,0:T(8,128)S(1)}, f32[2,384,128]{2,1,0:T(8,128)S(1)}, u32[]{:S(2)}, u32[]{:S(2)}) collective-permute-start(f32[2,384,128]{2,1,0:T(8,128)S(1)} %pad_maximum_fusion.9), channel_id=1, source_target_pairs={{1,0},{2,1},{3,2},{5,4},{6,5},{7,6},{9,8},{10,9},{11,10},{13,12},{... | collective-permute-start | bytes 1179656 | tf_op jit(solution)/shard_map/ppermute | solution.py:30
  180.1 28.8 %copy-start.7 = (f32[2,128,128]{2,1,0:T(8,128)S(1)}, f32[2,128,128]{2,1,0:T(8,128)}, u32[]{:S(2)}) copy-start(f32[2,128,128]{2,1,0:T(8,128)} %copy-done.6) | copy-start | bytes 393220
  180.1 28.7 %copy-start.12 = (f32[128,128]{1,0:T(8,128)S(1)}, f32[128,128]{1,0:T(8,128)}, u32[]{:S(2)}) copy-start(f32[128,128]{1,0:T(8,128)} %copy-done.11) | copy-start | bytes 196612
  180.2 10.6 %collective-permute-start.16 = (f32[2,128,384]{2,1,0:T(8,128)S(1)}, f32[2,128,384]{2,1,0:T(8,128)S(1)}, u32[]{:S(2)}, u32[]{:S(2)}) collective-permute-start(f32[2,128,384]{2,1,0:T(8,128)S(1)} %get-tuple-element.351), channel_id=1, source_target_pairs={{4,0},{8,4},{12,8},{16,12},{20,16},{24,20},{28,24},{5,1},{9,5},{13... | collective-permute-start | bytes 1179656 | tf_op jit(solution)/shard_map/ppermute | solution.py:17
  181.5 21.7 %collective-permute-start.17 = (f32[2,128,384]{2,1,0:T(8,128)S(1)}, f32[2,128,384]{2,1,0:T(8,128)S(1)}, u32[]{:S(2)}, u32[]{:S(2)}) collective-permute-start(f32[2,128,384]{2,1,0:T(8,128)S(1)} %get-tuple-element.352), channel_id=1, source_target_pairs={{0,4},{4,8},{8,12},{12,16},{16,20},{20,24},{24,28},{1,5},{5,9},{9,... | collective-permute-start | bytes 1179656 | tf_op jit(solution)/shard_map/ppermute | solution.py:17
  203.2 4.6 %collective-permute-start.18 = (f32[2,128,128]{2,1,0:T(8,128)S(1)}, f32[2,128,128]{2,1,0:T(8,128)S(1)}, u32[]{:S(2)}, u32[]{:S(2)}) collective-permute-start(f32[2,128,128]{2,1,0:T(8,128)S(1)} %get-tuple-element.366), channel_id=1, source_target_pairs={{1,0},{2,1},{3,2},{5,4},{6,5},{7,6},{9,8},{10,9},{11,10},{13,12},{... | collective-permute-start | bytes 393224 | tf_op jit(solution)/shard_map/ppermute | solution.py:17
  204.5 4.3 %collective-permute-start.19 = (f32[2,128,128]{2,1,0:T(8,128)S(1)}, f32[2,128,128]{2,1,0:T(8,128)S(1)}, u32[]{:S(2)}, u32[]{:S(2)}) collective-permute-start(f32[2,128,128]{2,1,0:T(8,128)S(1)} %get-tuple-element.367), channel_id=1, source_target_pairs={{0,1},{1,2},{2,3},{4,5},{5,6},{6,7},{8,9},{9,10},{10,11},{12,13},{... | collective-permute-start | bytes 393224 | tf_op jit(solution)/shard_map/ppermute | solution.py:17
  208.9 22.1 %copy-start.4 = (f32[2,128,128]{2,1,0:T(8,128)}, f32[2,128,128]{2,1,0:T(8,128)S(1)}, u32[]{:S(2)}) copy-start(f32[2,128,128]{2,1,0:T(8,128)S(1)} %fusion.60) | copy-start | bytes 393220
  208.9 6.6 %collective-permute-start.20 = (f32[2,128,128]{2,1,0:T(8,128)S(1)}, f32[2,128,128]{2,1,0:T(8,128)S(1)}, u32[]{:S(2)}, u32[]{:S(2)}) collective-permute-start(f32[2,128,128]{2,1,0:T(8,128)S(1)} %fusion.60), channel_id=1, source_target_pairs={{0,4},{4,8},{8,12},{12,16},{16,20},{20,24},{24,28},{1,5},{5,9},{9,... | collective-permute-start | bytes 393224 | tf_op jit(solution)/shard_map/ppermute | solution.py:28
  213.0 6.9 %collective-permute-start.21 = (f32[2,128,128]{2,1,0:T(8,128)S(1)}, f32[2,128,128]{2,1,0:T(8,128)S(1)}, u32[]{:S(2)}, u32[]{:S(2)}) collective-permute-start(f32[2,128,128]{2,1,0:T(8,128)S(1)} %fusion.60), channel_id=1, source_target_pairs={{4,0},{8,4},{12,8},{16,12},{20,16},{24,20},{28,24},{5,1},{9,5},{13... | collective-permute-start | bytes 393224 | tf_op jit(solution)/shard_map/ppermute | solution.py:30
  219.9 4.7 %collective-permute-start.22 = (f32[2,384,128]{2,1,0:T(8,128)S(1)}, f32[2,384,128]{2,1,0:T(8,128)S(1)}, u32[]{:S(2)}, u32[]{:S(2)}) collective-permute-start(f32[2,384,128]{2,1,0:T(8,128)S(1)} %pad_maximum_fusion.10), channel_id=1, source_target_pairs={{0,1},{1,2},{2,3},{4,5},{5,6},{6,7},{8,9},{9,10},{10,11},{12,13},{... | collective-permute-start | bytes 1179656 | tf_op jit(solution)/shard_map/ppermute | solution.py:28
  223.1 7.2 %collective-permute-start.23 = (f32[2,384,128]{2,1,0:T(8,128)S(1)}, f32[2,384,128]{2,1,0:T(8,128)S(1)}, u32[]{:S(2)}, u32[]{:S(2)}) collective-permute-start(f32[2,384,128]{2,1,0:T(8,128)S(1)} %pad_maximum_fusion.10), channel_id=1, source_target_pairs={{1,0},{2,1},{3,2},{5,4},{6,5},{7,6},{9,8},{10,9},{11,10},{13,12},{... | collective-permute-start | bytes 1179656 | tf_op jit(solution)/shard_map/ppermute | solution.py:30
  251.6 7.8 %copy-start.3 = (f32[1,4,256,256]{3,1,2,0:T(4,128)S(1)}, f32[1,4,256,256]{3,1,2,0:T(4,128)}, u32[]{:S(2)}) copy-start(f32[1,4,256,256]{3,1,2,0:T(4,128)} %copy.86) | copy-start | bytes 3145732
  252.6 10.8 %collective-permute-start.24 = (f32[2,128,384]{2,1,0:T(8,128)}, f32[2,128,384]{2,1,0:T(8,128)}, u32[]{:S(2)}, u32[]{:S(2)}) collective-permute-start(f32[2,128,384]{2,1,0:T(8,128)} %get-tuple-element.349), channel_id=1, source_target_pairs={{4,0},{8,4},{12,8},{16,12},{20,16},{24,20},{28,24},{5,1},{9,5},{13... | collective-permute-start | bytes 1179656 | tf_op jit(solution)/shard_map/ppermute | solution.py:17
  253.9 20.2 %collective-permute-start.25 = (f32[2,128,384]{2,1,0:T(8,128)}, f32[2,128,384]{2,1,0:T(8,128)}, u32[]{:S(2)}, u32[]{:S(2)}) collective-permute-start(f32[2,128,384]{2,1,0:T(8,128)} %get-tuple-element.350), channel_id=1, source_target_pairs={{0,4},{4,8},{8,12},{12,16},{16,20},{20,24},{24,28},{1,5},{5,9},{9,... | collective-permute-start | bytes 1179656 | tf_op jit(solution)/shard_map/ppermute | solution.py:17
  275.3 10.6 %collective-permute-start.26 = (f32[2,128,128]{2,1,0:T(8,128)S(1)}, f32[2,128,128]{2,1,0:T(8,128)S(1)}, u32[]{:S(2)}, u32[]{:S(2)}) collective-permute-start(f32[2,128,128]{2,1,0:T(8,128)S(1)} %get-tuple-element.364), channel_id=1, source_target_pairs={{1,0},{2,1},{3,2},{5,4},{6,5},{7,6},{9,8},{10,9},{11,10},{13,12},{... | collective-permute-start | bytes 393224 | tf_op jit(solution)/shard_map/ppermute | solution.py:17
  276.6 9.3 %collective-permute-start.27 = (f32[2,128,128]{2,1,0:T(8,128)S(1)}, f32[2,128,128]{2,1,0:T(8,128)S(1)}, u32[]{:S(2)}, u32[]{:S(2)}) collective-permute-start(f32[2,128,128]{2,1,0:T(8,128)S(1)} %get-tuple-element.365), channel_id=1, source_target_pairs={{0,1},{1,2},{2,3},{4,5},{5,6},{6,7},{8,9},{9,10},{10,11},{12,13},{... | collective-permute-start | bytes 393224 | tf_op jit(solution)/shard_map/ppermute | solution.py:17
  283.5 2.4 copy-start.5
  283.6 2.4 copy-start.13
  (12 other events, 12.0 us)
Sparse Core Ops, SparseCore 0:
  263.5 147.2 all-reduce.1
where the time goes:
time: 434 us; the launch traced here: 428 us
  waiting for transfers between devices  179 us (41%)
  starting transfers between devices  78 us (18%)
  blocking collectives  46.3 us (11%)
  local copies, waits for them, and re-layouts  44.9 us (10%)
  other arithmetic  38.7 us (9%)
  matrix products  23.7 us (5%)
  between operations  17.9 us (4%)
    psum x1, waiting for transfers between devices, local(): summed = lax.psum(terms, ('row', 'col'))  124 us
    ppermute x16, starting transfers between devices, passed_along(): return lax.ppermute(array, axis, pairs)  49.6 us
    pmax x1, blocking collectives, local(): peak = lax.pmax(jnp.max(light), ('row', 'col'))  46.3 us
    ppermute x16, waiting for transfers between devices, passed_along(): return lax.ppermute(array, axis, pairs)  28.8 us
    ppermute x6, waiting for transfers between devices, with_halo(): lax.ppermute(head, axis, [((i + 1) % count, i) for i in range(ends)])  22.1 us
    ppermute x6, starting transfers between devices, with_halo(): lax.ppermute(tail, axis, [(i, (i + 1) % count) for i in range(ends)])  20.4 us
    dynamic_update_slice x4, local copies, waits for them, and re-layouts, place(): return lax.dynamic_update_slice(buffer, piece, start)  19 us
    unnamed x72, local copies, waits for them, and re-layouts  13.4 us
  transfers between devices with their start and end apart: 29, of which 14 were waited for; matrix products, arithmetic and copies ran while one was open for 8% of the time, Pallas kernels for 0%

commit v1 on v0

--- a/solution.py
+++ b/solution.py
@@ -154,7 +154,7 @@
     probe_flat = jnp.concatenate(
         [probe_re.reshape(modes, pixels), probe_im.reshape(modes, pixels)], axis=0
     )
-    summed = lax.psum(terms, ("row", "col"))
+    summed = lax.psum(lax.psum(terms, "row"), "col")
     scale = probe_step / (summed[2 * modes] + mass_ratio * jnp.mean(summed[2 * modes]))
     updated = probe_flat + summed[: 2 * modes] * scale[None]
     new_re = updated[:modes].reshape(modes, width, width)

time: 434 us -> 525 us (1.21)
  waiting for transfers between devices: 179 us -> 277 us
    psum x1 -> x2, waiting for transfers between devices: 124 us -> 233 us  [local(): summed = lax.psum(lax.psum(terms, 'row'), 'col')]
    ppermute x16, waiting for transfers between devices: 28.8 us -> 18.1 us  [passed_along(): return lax.ppermute(array, axis, pairs)]
    unnamed x72 -> x70, local copies, waits for them, and re-layouts: 13.4 us -> 11.5 us
  transfers between devices with their start and end apart: 29 -> 30, of which waited for: 14 -> 14; matrix products, arithmetic and copies ran while one was open for 8% -> 7% of each run, Pallas kernels for 0% -> 0%
where the time goes in v1:
time: 525 us; the launch traced here: 519 us
  waiting for transfers between devices  277 us (53%)
  starting transfers between devices  74.2 us (14%)
  blocking collectives  46.3 us (9%)
  local copies, waits for them, and re-layouts  43 us (8%)
  other arithmetic  37.4 us (7%)
  matrix products  23.7 us (5%)
  between operations  17.9 us (3%)
    psum x2, waiting for transfers between devices, local(): summed = lax.psum(lax.psum(terms, 'row'), 'col')  233 us
    pmax x1, blocking collectives, local(): peak = lax.pmax(jnp.max(light), ('row', 'col'))  46.3 us
    ppermute x16, starting transfers between devices, passed_along(): return lax.ppermute(array, axis, pairs)  45.5 us
    ppermute x6, waiting for transfers between devices, with_halo(): lax.ppermute(head, axis, [((i + 1) % count, i) for i in range(ends)])  22.1 us
    ppermute x6, starting transfers between devices, with_halo(): lax.ppermute(tail, axis, [(i, (i + 1) % count) for i in range(ends)])  20.4 us
    dynamic_update_slice x4, local copies, waits for them, and re-layouts, place(): return lax.dynamic_update_slice(buffer, piece, start)  19 us
    ppermute x16, waiting for transfers between devices, passed_along(): return lax.ppermute(array, axis, pairs)  18.1 us
    unnamed x70, local copies, waits for them, and re-layouts  11.5 us
  transfers between devices with their start and end apart: 30, of which 14 were waited for; matrix products, arithmetic and copies ran while one was open for 7% of the time, Pallas kernels for 0%

profile of v1, /device:TPU:0, one launch (start us, length us, event | category | flops | bytes accessed | tf_op | source)
XLA Modules:
  0.0 519.0 jit_solution(1071666385682035322)
XLA Ops:
  8.3 4.9 collective-permute-start
  14.4 1.7 fusion.77
  16.1 3.9 collective-permute-done.1
  20.0 1.7 pad_maximum_fusion.8
  21.7 2.0 collective-permute-start.2
  32.4 1.6 multiply_convert_fusion.7
  34.1 1.8 fusion.32
  37.8 1.4 convolution_bitcast_fusion.10
  42.3 2.8 convolution_bitcast_fusion.8
  45.0 2.7 convolution_bitcast_fusion.9
  48.6 2.6 dynamic_update_slice.13
  51.2 1.8 fusion.151
  54.3 5.7 %collective-permute-start.9 = (f32[1,128,384]{2,1,0:T(8,128)}, f32[1,128,384]{2,1,0:T(8,128)}, u32[]{:S(2)}, u32[]{:S(2)}) collective-permute-start(f32[1,128,384]{2,1,0:T(8,128)} %get-tuple-element.356), channel_id=1, source_target_pairs={{0,4},{4,8},{8,12},{12,16},{16,20},{20,24},{24,28},{1,5},{5,9},{9,... | collective-permute-start | bytes 589832 | tf_op jit(solution)/shard_map/ppermute | solution.py:17
  60.0 3.0 add_reduce_fusion.5
  63.8 2.1 copy.48
  67.0 4.6 dynamic_update_slice.12
  71.6 2.1 fusion.150
  75.0 5.5 %collective-permute-start.5 = (f32[2,128,384]{2,1,0:T(8,128)}, f32[2,128,384]{2,1,0:T(8,128)}, u32[]{:S(2)}, u32[]{:S(2)}) collective-permute-start(f32[2,128,384]{2,1,0:T(8,128)} %get-tuple-element.354), channel_id=1, source_target_pairs={{0,4},{4,8},{8,12},{12,16},{16,20},{20,24},{24,28},{1,5},{5,9},{9,... | collective-permute-start | bytes 1179656 | tf_op jit(solution)/shard_map/ppermute | solution.py:17
  83.0 3.8 collective-permute-start.11
  88.3 46.3 %pmax.7 = f32[]{:T(128)} all-reduce(f32[]{:T(128)} %fusion.146), channel_id=1, replica_groups=mesh['row'=8,'col'=4] {'row','col'}, use_global_device_ids=true, to_apply=%region_5.6 | all-reduce | flops 1 | bytes 8 | tf_op jit(solution)/shard_map/pmax | solution.py:120
  137.9 3.0 collective-permute-start.7
  142.8 4.2 collective-permute-start.12
  148.3 2.6 collective-permute-done.12
  150.9 4.4 collective-permute-done.13
  155.3 2.0 collective-permute-start.14
  158.6 3.7 collective-permute-done.15
  164.8 1.4 convolution_bitcast_fusion.6
  169.7 1.4 convolution_bitcast_fusion.4
  174.2 5.9 %dynamic_update_slice.14 = f32[2,384,384]{2,1,0:T(8,128)S(1)} dynamic-update-slice(f32[2,384,384]{2,1,0:T(8,128)S(1)} %broadcast.616.clone.1, f32[2,256,256]{2,1,0:T(8,128)} %copy.58, s32[]{:T(128)} %constant.548.clone.1, s32[]{:T(128)S(6)} %select_n.65, s32[]{:T(128)S(6)} %select_n.66) | dynamic-update-slice | bytes 1048580 | tf_op jit(solution)/shard_map/dynamic_update_slice | solution.py:75
  181.5 5.5 %collective-permute-start.17 = (f32[2,128,384]{2,1,0:T(8,128)S(1)}, f32[2,128,384]{2,1,0:T(8,128)S(1)}, u32[]{:S(2)}, u32[]{:S(2)}) collective-permute-start(f32[2,128,384]{2,1,0:T(8,128)S(1)} %get-tuple-element.352), channel_id=1, source_target_pairs={{0,4},{4,8},{8,12},{12,16},{16,20},{20,24},{24,28},{1,5},{5,9},{9,... | collective-permute-start | bytes 1179656 | tf_op jit(solution)/shard_map/ppermute | solution.py:17
  187.0 3.8 collective-permute-done.16
  190.8 12.4 %collective-permute-done.17 = f32[2,128,384]{2,1,0:T(8,128)S(1)} collective-permute-done((f32[2,128,384]{2,1,0:T(8,128)S(1)}, f32[2,128,384]{2,1,0:T(8,128)S(1)}, u32[]{:S(2)}, u32[]{:S(2)}) %collective-permute-start.17) | collective-permute-done | bytes 393248 | tf_op jit(solution)/shard_map/ppermute | solution.py:17
  204.6 3.3 collective-permute-start.19
  208.9 4.1 collective-permute-start.20
  215.5 4.4 collective-permute-done.21
  219.9 3.2 collective-permute-start.22
  223.1 1.5 collective-permute-start.23
  224.6 5.7 %collective-permute-done.23 = f32[2,384,128]{2,1,0:T(8,128)S(1)} collective-permute-done((f32[2,384,128]{2,1,0:T(8,128)S(1)}, f32[2,384,128]{2,1,0:T(8,128)S(1)}, u32[]{:S(2)}, u32[]{:S(2)}) %collective-permute-start.23) | collective-permute-done | bytes 393248 | tf_op jit(solution)/shard_map/ppermute | solution.py:30
  242.9 2.7 pad_maximum_fusion
  246.8 5.9 %dynamic_update_slice.15 = f32[2,384,384]{2,1,0:T(8,128)S(1)} dynamic-update-slice(f32[2,384,384]{2,1,0:T(8,128)S(1)} %broadcast.616, f32[2,256,256]{2,1,0:T(8,128)} %pad_maximum_fusion.7, s32[]{:T(128)} %constant.548.clone.1, s32[]{:T(128)S(6)} %select_n.65, s32[]{:T(128)S(6)} %select_n.66) | dynamic-update-slice | bytes 1048580 | tf_op jit(solution)/shard_map/dynamic_update_slice | solution.py:75
  255.0 5.3 %collective-permute-start.25 = (f32[2,128,384]{2,1,0:T(8,128)}, f32[2,128,384]{2,1,0:T(8,128)}, u32[]{:S(2)}, u32[]{:S(2)}) collective-permute-start(f32[2,128,384]{2,1,0:T(8,128)} %get-tuple-element.350), channel_id=1, source_target_pairs={{0,4},{4,8},{8,12},{12,16},{16,20},{20,24},{24,28},{1,5},{5,9},{9,... | collective-permute-start | bytes 1179656 | tf_op jit(solution)/shard_map/ppermute | solution.py:17
  260.3 154.3 %all-reduce.3.cloned.1.call-done = f32[9,65536]{1,0:T(8,128)} async-done(((f32[9,65536]{1,0:T(8,128)}), f32[9,65536]{1,0:T(8,128)}) %all-reduce.3.cloned.1.call-update) | async-done | bytes 2359312 | tf_op jit(solution)/shard_map/psum | solution.py:157
  417.2 3.0 collective-permute-start.27
  420.9 1.6 copy.84
  423.3 78.2 %all-reduce.5.cloned.1.call-done = f32[9,65536]{1,0:T(8,128)} async-done(((f32[9,65536]{1,0:T(8,128)}), f32[9,65536]{1,0:T(8,128)}) %all-reduce.5.cloned.1.call-update) | async-done | bytes 2359312 | tf_op jit(solution)/shard_map/psum | solution.py:157
  501.5 2.7 slice_reduce_fusion
  504.9 1.9 add_divide_fusion
  506.8 2.5 fusion
  (170 shorter events, 68.5 us)
Async XLA Ops:
  7.2 21.6 %copy-start = (f32[4,256,256]{2,1,0:T(8,128)S(1)}, f32[4,256,256]{2,1,0:T(8,128)}, u32[]{:S(2)}) copy-start(f32[4,256,256]{2,1,0:T(8,128)} %param.72) | copy-start | bytes 3145732
  7.2 21.9 %copy-start.1 = (f32[4,256,256]{2,1,0:T(8,128)S(1)}, f32[4,256,256]{2,1,0:T(8,128)}, u32[]{:S(2)}) copy-start(f32[4,256,256]{2,1,0:T(8,128)} %param.73) | copy-start | bytes 3145732
  7.2 407.4 %all-reduce.3.cloned.1.call-start = ((), (), s32[]{:S(2)}) async-start(), calls=%async_computation | async-start | bytes 8388608 | tf_op jit(solution)/shard_map/psum | solution.py:157
  8.3 7.8 %collective-permute-start = (f32[2,128,128]{2,1,0:T(8,128)S(1)}, f32[2,128,128]{2,1,0:T(8,128)S(1)}, u32[]{:S(2)}, u32[]{:S(2)}) collective-permute-start(f32[2,128,128]{2,1,0:T(8,128)S(1)} %pad_maximum_fusion.11), channel_id=1, source_target_pairs={{0,4},{4,8},{8,12},{12,16},{16,20},{20,24},{24,28},{1,5},{5,9},{9,... | collective-permute-start | bytes 393224 | tf_op jit(solution)/shard_map/ppermute | solution.py:28
  13.1 6.9 %collective-permute-start.1 = (f32[2,128,128]{2,1,0:T(8,128)S(1)}, f32[2,128,128]{2,1,0:T(8,128)S(1)}, u32[]{:S(2)}, u32[]{:S(2)}) collective-permute-start(f32[2,128,128]{2,1,0:T(8,128)S(1)} %pad_maximum_fusion.11), channel_id=1, source_target_pairs={{4,0},{8,4},{12,8},{16,12},{20,16},{24,20},{28,24},{5,1},{9,5},{13... | collective-permute-start | bytes 393224 | tf_op jit(solution)/shard_map/ppermute | solution.py:30
  16.1 3.9 copy-start.13
  20.0 1.7 copy-start.14
  21.7 12.4 %collective-permute-start.2 = (f32[2,384,128]{2,1,0:T(8,128)}, f32[2,384,128]{2,1,0:T(8,128)}, u32[]{:S(2)}, u32[]{:S(2)}) collective-permute-start(f32[2,384,128]{2,1,0:T(8,128)} %pad_maximum_fusion.8), channel_id=1, source_target_pairs={{0,1},{1,2},{2,3},{4,5},{5,6},{6,7},{8,9},{9,10},{10,11},{12,13},{... | collective-permute-start | bytes 1179656 | tf_op jit(solution)/shard_map/ppermute | solution.py:28
  23.7 10.4 %collective-permute-start.3 = (f32[2,384,128]{2,1,0:T(8,128)}, f32[2,384,128]{2,1,0:T(8,128)}, u32[]{:S(2)}, u32[]{:S(2)}) collective-permute-start(f32[2,384,128]{2,1,0:T(8,128)} %pad_maximum_fusion.8), channel_id=1, source_target_pairs={{1,0},{2,1},{3,2},{5,4},{6,5},{7,6},{9,8},{10,9},{11,10},{13,12},{... | collective-permute-start | bytes 1179656 | tf_op jit(solution)/shard_map/ppermute | solution.py:30
  28.7 5.4 %copy-start.8 = (f32[128,128]{1,0:T(8,128)S(1)}, f32[128,128]{1,0:T(8,128)}, u32[]{:S(2)}) copy-start(f32[128,128]{1,0:T(8,128)} %param.71) | copy-start | bytes 196612
  28.8 5.4 %copy-start.9 = (f32[128,128]{1,0:T(8,128)S(1)}, f32[128,128]{1,0:T(8,128)}, u32[]{:S(2)}) copy-start(f32[128,128]{1,0:T(8,128)} %param.70) | copy-start | bytes 196612
  31.4 10.1 %copy-start.18 = (bf16[256,256]{1,0:T(8,128)(2,1)}, bf16[256,256]{1,0:T(8,128)(2,1)S(1)}, u32[]{:S(2)}) copy-start(bf16[256,256]{1,0:T(8,128)(2,1)S(1)} %fusion.78) | copy-start | bytes 393220
  32.4 9.1 %copy-start.21 = (bf16[256,256]{1,0:T(8,128)(2,1)}, bf16[256,256]{1,0:T(8,128)(2,1)S(1)}, u32[]{:S(2)}) copy-start(bf16[256,256]{1,0:T(8,128)(2,1)S(1)} %multiply_convert_fusion.6) | copy-start | bytes 393220
  34.1 3.0 copy-start.27
  34.1 7.4 %copy-start.24 = (bf16[256,256]{1,0:T(8,128)(2,1)}, bf16[256,256]{1,0:T(8,128)(2,1)S(1)}, u32[]{:S(2)}) copy-start(bf16[256,256]{1,0:T(8,128)(2,1)S(1)} %get-tuple-element.377) | copy-start | bytes 393220
  53.0 27.5 %collective-permute-start.8 = (f32[1,128,384]{2,1,0:T(8,128)}, f32[1,128,384]{2,1,0:T(8,128)}, u32[]{:S(2)}, u32[]{:S(2)}) collective-permute-start(f32[1,128,384]{2,1,0:T(8,128)} %get-tuple-element.355), channel_id=1, source_target_pairs={{4,0},{8,4},{12,8},{16,12},{20,16},{24,20},{28,24},{5,1},{9,5},{13... | collective-permute-start | bytes 589832 | tf_op jit(solution)/shard_map/ppermute | solution.py:17
  54.3 26.2 %collective-permute-start.9 = (f32[1,128,384]{2,1,0:T(8,128)}, f32[1,128,384]{2,1,0:T(8,128)}, u32[]{:S(2)}, u32[]{:S(2)}) collective-permute-start(f32[1,128,384]{2,1,0:T(8,128)} %get-tuple-element.356), channel_id=1, source_target_pairs={{0,4},{4,8},{8,12},{12,16},{16,20},{20,24},{24,28},{1,5},{5,9},{9,... | collective-permute-start | bytes 589832 | tf_op jit(solution)/shard_map/ppermute | solution.py:17
  73.7 61.5 %collective-permute-start.4 = (f32[2,128,384]{2,1,0:T(8,128)}, f32[2,128,384]{2,1,0:T(8,128)}, u32[]{:S(2)}, u32[]{:S(2)}) collective-permute-start(f32[2,128,384]{2,1,0:T(8,128)} %get-tuple-element.353), channel_id=1, source_target_pairs={{4,0},{8,4},{12,8},{16,12},{20,16},{24,20},{28,24},{5,1},{9,5},{13... | collective-permute-start | bytes 1179656 | tf_op jit(solution)/shard_map/ppermute | solution.py:17
  75.0 60.3 %collective-permute-start.5 = (f32[2,128,384]{2,1,0:T(8,128)}, f32[2,128,384]{2,1,0:T(8,128)}, u32[]{:S(2)}, u32[]{:S(2)}) collective-permute-start(f32[2,128,384]{2,1,0:T(8,128)} %get-tuple-element.354), channel_id=1, source_target_pairs={{0,4},{4,8},{8,12},{12,16},{16,20},{20,24},{24,28},{1,5},{5,9},{9,... | collective-permute-start | bytes 1179656 | tf_op jit(solution)/shard_map/ppermute | solution.py:17
  81.7 6.0 %copy-start.7 = (f32[1,128,384]{2,1,0:T(8,128)}, f32[1,128,384]{2,1,0:T(8,128)S(1)}, u32[]{:S(2)}) copy-start(f32[1,128,384]{2,1,0:T(8,128)S(1)} %fusion.48) | copy-start | bytes 589828
  81.7 5.1 collective-permute-start.10
  83.0 4.6 collective-permute-start.11
  136.6 5.2 %collective-permute-start.6 = (f32[2,128,128]{2,1,0:T(8,128)S(1)}, f32[2,128,128]{2,1,0:T(8,128)S(1)}, u32[]{:S(2)}, u32[]{:S(2)}) collective-permute-start(f32[2,128,128]{2,1,0:T(8,128)S(1)} %get-tuple-element.368), channel_id=1, source_target_pairs={{1,0},{2,1},{3,2},{5,4},{6,5},{7,6},{9,8},{10,9},{11,10},{13,12},{... | collective-permute-start | bytes 393224 | tf_op jit(solution)/shard_map/ppermute | solution.py:17
  137.9 4.0 collective-permute-start.7
  141.8 9.1 %copy-start.10 = (f32[128,128]{1,0:T(8,128)}, f32[128,128]{1,0:T(8,128)S(1)}, u32[]{:S(2)}) copy-start(f32[128,128]{1,0:T(8,128)S(1)} %add_bitcast_fusion.2) | copy-start | bytes 196612
  142.8 20.6 %copy-start.5 = (f32[2,128,128]{2,1,0:T(8,128)}, f32[2,128,128]{2,1,0:T(8,128)S(1)}, u32[]{:S(2)}) copy-start(f32[2,128,128]{2,1,0:T(8,128)S(1)} %fusion.63) | copy-start | bytes 393220
  142.8 8.1 %collective-permute-start.12 = (f32[2,128,128]{2,1,0:T(8,128)S(1)}, f32[2,128,128]{2,1,0:T(8,128)S(1)}, u32[]{:S(2)}, u32[]{:S(2)}) collective-permute-start(f32[2,128,128]{2,1,0:T(8,128)S(1)} %fusion.63), channel_id=1, source_target_pairs={{0,4},{4,8},{8,12},{12,16},{16,20},{20,24},{24,28},{1,5},{5,9},{9,... | collective-permute-start | bytes 393224 | tf_op jit(solution)/shard_map/ppermute | solution.py:28
  147.0 8.2 %collective-permute-start.13 = (f32[2,128,128]{2,1,0:T(8,128)S(1)}, f32[2,128,128]{2,1,0:T(8,128)S(1)}, u32[]{:S(2)}, u32[]{:S(2)}) collective-permute-start(f32[2,128,128]{2,1,0:T(8,128)S(1)} %fusion.63), channel_id=1, source_target_pairs={{4,0},{8,4},{12,8},{16,12},{20,16},{24,20},{28,24},{5,1},{9,5},{13... | collective-permute-start | bytes 393224 | tf_op jit(solution)/shard_map/ppermute | solution.py:30
  155.3 3.4 collective-permute-start.14
  157.3 5.1 collective-permute-start.15
  180.1 28.8 %copy-start.6 = (f32[2,128,128]{2,1,0:T(8,128)S(1)}, f32[2,128,128]{2,1,0:T(8,128)}, u32[]{:S(2)}) copy-start(f32[2,128,128]{2,1,0:T(8,128)} %copy-done.5) | copy-start | bytes 393220
  180.1 28.7 %copy-start.11 = (f32[128,128]{1,0:T(8,128)S(1)}, f32[128,128]{1,0:T(8,128)}, u32[]{:S(2)}) copy-start(f32[128,128]{1,0:T(8,128)} %copy-done.10) | copy-start | bytes 196612
  180.2 10.6 %collective-permute-start.16 = (f32[2,128,384]{2,1,0:T(8,128)S(1)}, f32[2,128,384]{2,1,0:T(8,128)S(1)}, u32[]{:S(2)}, u32[]{:S(2)}) collective-permute-start(f32[2,128,384]{2,1,0:T(8,128)S(1)} %get-tuple-element.351), channel_id=1, source_target_pairs={{4,0},{8,4},{12,8},{16,12},{20,16},{24,20},{28,24},{5,1},{9,5},{13... | collective-permute-start | bytes 1179656 | tf_op jit(solution)/shard_map/ppermute | solution.py:17
  181.5 21.7 %collective-permute-start.17 = (f32[2,128,384]{2,1,0:T(8,128)S(1)}, f32[2,128,384]{2,1,0:T(8,128)S(1)}, u32[]{:S(2)}, u32[]{:S(2)}) collective-permute-start(f32[2,128,384]{2,1,0:T(8,128)S(1)} %get-tuple-element.352), channel_id=1, source_target_pairs={{0,4},{4,8},{8,12},{12,16},{16,20},{20,24},{24,28},{1,5},{5,9},{9,... | collective-permute-start | bytes 1179656 | tf_op jit(solution)/shard_map/ppermute | solution.py:17
  203.3 4.6 collective-permute-start.18
  204.6 4.3 collective-permute-start.19
  208.9 22.1 %copy-start.3 = (f32[2,128,128]{2,1,0:T(8,128)}, f32[2,128,128]{2,1,0:T(8,128)S(1)}, u32[]{:S(2)}) copy-start(f32[2,128,128]{2,1,0:T(8,128)S(1)} %fusion.60) | copy-start | bytes 393220
  208.9 6.6 %collective-permute-start.20 = (f32[2,128,128]{2,1,0:T(8,128)S(1)}, f32[2,128,128]{2,1,0:T(8,128)S(1)}, u32[]{:S(2)}, u32[]{:S(2)}) collective-permute-start(f32[2,128,128]{2,1,0:T(8,128)S(1)} %fusion.60), channel_id=1, source_target_pairs={{0,4},{4,8},{8,12},{12,16},{16,20},{20,24},{24,28},{1,5},{5,9},{9,... | collective-permute-start | bytes 393224 | tf_op jit(solution)/shard_map/ppermute | solution.py:28
  213.0 6.9 %collective-permute-start.21 = (f32[2,128,128]{2,1,0:T(8,128)S(1)}, f32[2,128,128]{2,1,0:T(8,128)S(1)}, u32[]{:S(2)}, u32[]{:S(2)}) collective-permute-start(f32[2,128,128]{2,1,0:T(8,128)S(1)} %fusion.60), channel_id=1, source_target_pairs={{4,0},{8,4},{12,8},{16,12},{20,16},{24,20},{28,24},{5,1},{9,5},{13... | collective-permute-start | bytes 393224 | tf_op jit(solution)/shard_map/ppermute | solution.py:30
  219.9 4.7 collective-permute-start.22
  223.1 7.2 %collective-permute-start.23 = (f32[2,384,128]{2,1,0:T(8,128)S(1)}, f32[2,384,128]{2,1,0:T(8,128)S(1)}, u32[]{:S(2)}, u32[]{:S(2)}) collective-permute-start(f32[2,384,128]{2,1,0:T(8,128)S(1)} %pad_maximum_fusion.10), channel_id=1, source_target_pairs={{1,0},{2,1},{3,2},{5,4},{6,5},{7,6},{9,8},{10,9},{11,10},{13,12},{... | collective-permute-start | bytes 1179656 | tf_op jit(solution)/shard_map/ppermute | solution.py:30
  245.6 255.9 %all-reduce.5.cloned.1.call-start = ((), (), s32[]{:S(2)}) async-start(), calls=%async_computation.1 | async-start | bytes 8388608 | tf_op jit(solution)/shard_map/psum | solution.py:157
  253.7 161.0 %collective-permute-start.24 = (f32[2,128,384]{2,1,0:T(8,128)}, f32[2,128,384]{2,1,0:T(8,128)}, u32[]{:S(2)}, u32[]{:S(2)}) collective-permute-start(f32[2,128,384]{2,1,0:T(8,128)} %get-tuple-element.349), channel_id=1, source_target_pairs={{4,0},{8,4},{12,8},{16,12},{20,16},{24,20},{28,24},{5,1},{9,5},{13... | collective-permute-start | bytes 1179656 | tf_op jit(solution)/shard_map/ppermute | solution.py:17
  255.0 159.7 %collective-permute-start.25 = (f32[2,128,384]{2,1,0:T(8,128)}, f32[2,128,384]{2,1,0:T(8,128)}, u32[]{:S(2)}, u32[]{:S(2)}) collective-permute-start(f32[2,128,384]{2,1,0:T(8,128)} %get-tuple-element.350), channel_id=1, source_target_pairs={{0,4},{4,8},{8,12},{12,16},{16,20},{20,24},{24,28},{1,5},{5,9},{9,... | collective-permute-start | bytes 1179656 | tf_op jit(solution)/shard_map/ppermute | solution.py:17
  415.9 6.7 %collective-permute-start.26 = (f32[2,128,128]{2,1,0:T(8,128)S(1)}, f32[2,128,128]{2,1,0:T(8,128)S(1)}, u32[]{:S(2)}, u32[]{:S(2)}) collective-permute-start(f32[2,128,128]{2,1,0:T(8,128)S(1)} %get-tuple-element.364), channel_id=1, source_target_pairs={{1,0},{2,1},{3,2},{5,4},{6,5},{7,6},{9,8},{10,9},{11,10},{13,12},{... | collective-permute-start | bytes 393224 | tf_op jit(solution)/shard_map/ppermute | solution.py:17
  417.2 5.4 %collective-permute-start.27 = (f32[2,128,128]{2,1,0:T(8,128)S(1)}, f32[2,128,128]{2,1,0:T(8,128)S(1)}, u32[]{:S(2)}, u32[]{:S(2)}) collective-permute-start(f32[2,128,128]{2,1,0:T(8,128)S(1)} %get-tuple-element.365), channel_id=1, source_target_pairs={{0,1},{1,2},{2,3},{4,5},{5,6},{6,7},{8,9},{9,10},{10,11},{12,13},{... | collective-permute-start | bytes 393224 | tf_op jit(solution)/shard_map/ppermute | solution.py:17
  420.2 2.4 copy-start.4
  420.2 2.4 copy-start.12
  (12 other events, 12.1 us)
Sparse Core Ops, SparseCore 0:
  245.7 168.8 all-reduce.2
  417.0 84.4 all-reduce.4
